TPU v7x, 32 devices: a whole 2x2x4 slice. The times are simulated.
32 devices in a mesh: section: 2 (over y), wide: 8 (over z, core), narrow: 2 (over x).
Axes of the slice: x: 2, y: 2, z: 4, core: 2. Of those that a mesh axis runs over, the one named last changes fastest.
Arguments:
- hidden: bfloat16 [2, 1024, 24576], P('section', None, 'wide'), may hold values from -6 to 6
- down_weight: bfloat16 [12288, 24576], P('narrow', 'wide'), may hold values from -0.0390625 to 0.0390625
- residual: bfloat16 [2, 1024, 12288], P('section', None, 'narrow'), may hold values from -6 to 6
- ln_gain: float32 [12288], P('narrow'), may hold values from 0.5 to 1.5
- ln_bias: float32 [12288], P('narrow'), may hold values from -3 to 3
- qkv_weight: bfloat16 [12288, 24576], P('narrow', 'wide'), may hold values from -1 to 1
Outputs:
- stream: bfloat16 [2, 1024, 12288], P('section', 'wide', 'narrow')
- context: bfloat16 [2, 1024, 8192], P('section', 'narrow', 'wide')
All inputs are finite; a program needn't handle non-finite values.
Results may differ from a plain program's by a relative error of at most 0.007.
Values may be sent and summed in bfloat16 or wider, within the bound.
A program may use at most 320 MiB of HBM per device.

v0:
```python
import jax
import jax.numpy as jnp
from jax import lax
from jax.sharding import PartitionSpec as P

D = 12288
HDIM = 128


def from_behind(value, axis, steps):
    count = lax.axis_size(axis)
    pairs = [(source, (source + steps) % count) for source in range(count)]
    return lax.ppermute(value, axis, pairs)


def per_device(hidden, down_weight, residual, ln_gain, ln_bias, qkv_weight):
    inner = hidden[0]
    resid = residual[0]
    seq_len = inner.shape[0]
    wide_rows = seq_len // lax.axis_size("wide")
    wide_at = lax.axis_index("wide")
    contract = (((1,), (1,)), ((), ()))
    partial_ffn = lax.dot_general(inner, down_weight, contract, preferred_element_type=jnp.float32)
    summed = lax.psum(partial_ffn, "wide")
    mine = (resid.astype(jnp.float32) + summed).astype(jnp.bfloat16)
    arrived = from_behind(mine, "section", 1)
    own_rows = lax.dynamic_slice_in_dim(mine, wide_at * wide_rows, wide_rows, 0)
    values = arrived.astype(jnp.float32)
    totals, squares = lax.psum(
        (jnp.sum(values, axis=1), jnp.sum(values * values, axis=1)), "narrow"
    )
    mean = totals / D
    var = squares / D - mean * mean
    normed = (
        (values - mean[:, None]) * lax.rsqrt(var + 1e-05)[:, None] * ln_gain + ln_bias
    ).astype(jnp.bfloat16)
    heads_here = qkv_weight.shape[1] // (3 * HDIM)
    query_count = seq_len // lax.axis_size("narrow")
    narrow_at = lax.axis_index("narrow")
    joined = lax.psum(
        jnp.dot(normed, qkv_weight, preferred_element_type=jnp.float32), "narrow"
    ).astype(jnp.bfloat16)
    mine_joined = lax.dynamic_slice_in_dim(joined, narrow_at * query_count, query_count, 0)
    query = mine_joined.reshape(query_count, heads_here, 3, HDIM)[:, :, 0]
    pairs = joined.reshape(seq_len, heads_here, 3, HDIM)[:, :, 1:]
    keys = pairs[:, :, 0]
    vals = pairs[:, :, 1]
    scores = jnp.einsum("qhd,khd->hqk", query, keys, preferred_element_type=jnp.float32) / jnp.sqrt(
        jnp.float32(HDIM)
    )
    query_pos = narrow_at * query_count + lax.broadcasted_iota(jnp.int32, (query_count, seq_len), 0)
    key_pos = lax.broadcasted_iota(jnp.int32, (query_count, seq_len), 1)
    scores = jnp.where((key_pos <= query_pos)[None], scores, jnp.float32(-1e30))
    top = jnp.max(scores, axis=2, keepdims=True)
    expd = jnp.exp(scores - top)
    probs = (expd / jnp.sum(expd, axis=2, keepdims=True)).astype(jnp.bfloat16)
    attended = jnp.einsum("hqk,khd->qhd", probs, vals, preferred_element_type=jnp.float32).astype(
        jnp.bfloat16
    )
    attended = attended.reshape(query_count, heads_here * HDIM)
    return (own_rows[None], attended[None])


def solution(mesh):
    return jax.shard_map(
        per_device,
        mesh=mesh,
        in_specs=(
            P("section", None, "wide"),
            P("narrow", "wide"),
            P("section", None, "narrow"),
            P("narrow"),
            P("narrow"),
            P("narrow", "wide"),
        ),
        out_specs=(P("section", "wide", "narrow"), P("section", "narrow", "wide")),
        check_vma=False,
    )
```

profile of v0, /device:TPU:0, one launch (start us, length us, event | category | flops | bytes accessed | tf_op | source)
XLA Modules:
  0.0 1245.0 jit_solution(1324470787373891507)
XLA Ops:
  7.2 0.0 all-reduce.4.cloned.1.call-start
  7.2 46.9 %fusion.18 = f32[1024,6144]{1,0:T(8,128)} fusion(bf16[6144,3072]{1,0:T(8,128)(2,1)} %param.7, bf16[1,1024,3072]{2,1,0:T(8,128)(2,1)} %param.6), kind=kOutput, calls=%fused_computation.24 | convolution fusion | flops 38654705664 | bytes 69206016 | tf_op jit(solution)/shard_map/dot_general | solution.py:23
  54.1 0.0 all-reduce.4.cloned.1.call-update
  54.1 0.0 copy-start.1
  54.1 0.0 copy-start.2
  54.1 493.4 %all-reduce.4.cloned.1.call-done = f32[1024,6144]{1,0:T(8,128)} async-done(((f32[1024,6144]{1,0:T(8,128)}), f32[1024,6144]{1,0:T(8,128)}) %all-reduce.4.cloned.1.call-update) | async-done | bytes 25165840 | tf_op jit(solution)/shard_map/psum | solution.py:24
  547.5 17.2 %fusion.6 = bf16[1024,6144]{1,0:T(8,128)(2,1)} fusion(f32[1024,6144]{1,0:T(8,128)} %all-reduce.4.cloned.1.call-done, bf16[1,1024,6144]{2,1,0:T(8,128)(2,1)} %param.8), kind=kLoop, calls=%fused_computation.10 | loop fusion | flops 18874368 | bytes 50331648 | tf_op jit(solution)/shard_map/convert_element_type | solution.py:25
  564.7 1.5 collective-permute-start
  566.1 1.2 iota_compare_fusion
  567.3 2.7 dynamic-slice_bitcast_fusion
  570.0 266.8 %collective-permute-done = bf16[1024,6144]{1,0:T(8,128)(2,1)} collective-permute-done((bf16[1024,6144]{1,0:T(8,128)(2,1)}, bf16[1024,6144]{1,0:T(8,128)(2,1)}, u32[]{:S(2)}, u32[]{:S(2)}) %collective-permute-start) | collective-permute-done | bytes 12582944 | tf_op jit(solution)/shard_map/ppermute | solution.py:13
  836.8 8.5 convert_reduce_fusion
  845.3 5.0 all-reduce
  850.3 0.0 copy-done.1
  850.3 0.0 copy-done.2
  850.3 48.3 %fusion.8 = f32[1024,3072]{1,0:T(8,128)} fusion(bf16[6144,3072]{1,0:T(8,128)(2,1)} %param.11, bf16[1024,6144]{1,0:T(8,128)(2,1)} %collective-permute-done, f32[6144]{0:T(1024)S(1)} %copy-done.1, f32[6144]{0:T(1024)S(1)} %copy-done.2, f32[1024]{0:T(1024)S(1)} %get-tuple-element.11, f32[1024]{0:T(1024)S(1)} %get-tuple-element.10), kind=kOutput, calls=%fused_computation.15 | convolution fusion | flops 38692454400 | bytes 62971904 | tf_op jit(solution)/shard_map/dot_general | solution.py:41
  898.6 285.4 %all-reduce.5 = bf16[1024,3072]{1,0:T(8,128)(2,1)} all-reduce(f32[1024,3072]{1,0:T(8,128)} %fusion.8), channel_id=1, replica_groups=mesh['section'=2,'wide'=8,'narrow'=2] {'narrow'}, use_global_device_ids=true, to_apply=%region_5.0 | all-reduce | flops 3145728 | bytes 18874368 | tf_op jit(solution)/shard_map/psum | solution.py:40
  1184.0 8.6 copy.11
  1192.6 2.1 constant_dynamic-slice_fusion
  1194.7 2.8 copy.13
  1197.5 0.0 copy-start
  1197.5 10.1 fusion.20
  1207.6 0.0 copy-done
  1207.6 21.2 %fusion.24 = (f32[8,512]{1,0:T(8,128)S(1)}, f32[8,512,1024]{2,1,0:T(8,128)}) fusion(f32[8,512,1024]{2,1,0:T(8,128)} %fusion.20, pred[512,1024]{1,0:T(8,128)(4,1)S(1)} %copy-done), kind=kOutput, calls=%fused_computation.39 | output fusion | flops 25166848 | bytes 34095104 | tf_op jit(solution)/shard_map/sub | solution.py:55
  1228.8 8.0 fusion.21
  1236.9 1.3 copy.16
  (2 shorter events, 0.0 us)
Async XLA Ops:
  7.2 540.3 %all-reduce.4.cloned.1.call-start = ((), (), s32[]{:S(2)}) async-start(), calls=%async_computation | async-start | bytes 50331648 | tf_op jit(solution)/shard_map/psum | solution.py:24
  54.1 796.2 %copy-start.1 = (f32[6144]{0:T(1024)S(1)}, f32[6144]{0:T(1024)}, u32[]{:S(2)}) copy-start(f32[6144]{0:T(1024)} %param.10) | copy-start | bytes 73732
  54.1 796.2 %copy-start.2 = (f32[6144]{0:T(1024)S(1)}, f32[6144]{0:T(1024)}, u32[]{:S(2)}) copy-start(f32[6144]{0:T(1024)} %param.9) | copy-start | bytes 73732
  564.7 272.1 %collective-permute-start = (bf16[1024,6144]{1,0:T(8,128)(2,1)}, bf16[1024,6144]{1,0:T(8,128)(2,1)}, u32[]{:S(2)}, u32[]{:S(2)}) collective-permute-start(bf16[1024,6144]{1,0:T(8,128)(2,1)} %fusion.6), channel_id=1, source_target_pairs={{0,16},{16,0},{1,17},{17,1},{2,18},{18,2},{3,19},{19,3},{4,20},{20... | collective-permute-start | bytes 37748744 | tf_op jit(solution)/shard_map/ppermute | solution.py:13
  1197.5 10.1 copy-start
Sparse Core Ops, SparseCore 0:
  54.2 493.2 all-reduce.3
where the time goes:
time: 1250 us
  waiting for transfers between devices  760 us (61%)
  blocking collectives  290 us (23%)
  matrix products  113 us (9%)
  other arithmetic  48.1 us (4%)
  local copies, waits for them, and re-layouts  17.6 us (1%)
  between operations  14.1 us (1%)
    psum x1, waiting for transfers between devices, per_device(): summed = lax.psum(partial_ffn, 'wide')  493 us
    psum x1, blocking collectives, per_device(): lax.psum(jnp.dot(normed, qkv_weight, preferred_element_type=jnp.float32),...  285 us
    ppermute x1, waiting for transfers between devices, from_behind(): return lax.ppermute(value, axis, pairs)  267 us
    dot_general x1, matrix products, per_device(): jnp.dot(normed, qkv_weight, preferred_element_type=jnp.float32)  48.3 us
    dot_general x1, matrix products, per_device(): lax.dot_general(inner, down_weight, contract, preferred_element_type=jnp....  46.9 us
  transfers between devices with their start and end apart: 2, of which 2 were waited for; matrix products, arithmetic and copies ran while one was open for 0% of the time, Pallas kernels for 0%

commit v1 on v0

--- a/solution.py
+++ b/solution.py
@@ -1,10 +1,16 @@
+import functools
+
 import jax
 import jax.numpy as jnp
 from jax import lax
+from jax.experimental import pallas as pl
+from jax.experimental.pallas import tpu as pltpu
 from jax.sharding import PartitionSpec as P
 
 D = 12288
 HDIM = 128
+CHUNKS = 2
+QBLOCK = 256
 
 
 def from_behind(value, axis, steps):
@@ -13,7 +19,102 @@
     return lax.ppermute(value, axis, pairs)
 
 
-def per_device(hidden, down_weight, residual, ln_gain, ln_bias, qkv_weight):
+def attend_head(seq_len, joined_ref, out_ref):
+    block = min(QBLOCK, seq_len)
+    scale = 1.0 / (HDIM**0.5)
+    for start in range(0, seq_len, block):
+        stop = start + block
+        query = joined_ref[start:stop, :HDIM]
+        keys = joined_ref[:stop, HDIM : 2 * HDIM]
+        vals = joined_ref[:stop, 2 * HDIM :]
+        scores = (
+            lax.dot_general(query, keys, (((1,), (1,)), ((), ())), preferred_element_type=jnp.float32)
+            * scale
+        )
+        rows = start + lax.broadcasted_iota(jnp.int32, scores.shape, 0)
+        cols = lax.broadcasted_iota(jnp.int32, scores.shape, 1)
+        scores = jnp.where(cols <= rows, scores, jnp.float32(-1e30))
+        top = jnp.max(scores, axis=1, keepdims=True)
+        expd = jnp.exp(scores - top)
+        probs = (expd * (1.0 / jnp.sum(expd, axis=1, keepdims=True))).astype(jnp.bfloat16)
+        out_ref[start:stop, :] = jnp.dot(probs, vals, preferred_element_type=jnp.float32).astype(
+            jnp.bfloat16
+        )
+
+
+def attention(joined):
+    seq_len, width = joined.shape
+    heads = width // (3 * HDIM)
+    return pl.pallas_call(
+        functools.partial(attend_head, seq_len),
+        grid=(heads,),
+        in_specs=[pl.BlockSpec((seq_len, 3 * HDIM), lambda h: (0, h))],
+        out_specs=pl.BlockSpec((seq_len, HDIM), lambda h: (0, h)),
+        out_shape=jax.ShapeDtypeStruct((seq_len, heads * HDIM), jnp.bfloat16),
+        compiler_params=pltpu.CompilerParams(vmem_limit_bytes=32 << 20),
+        cost_estimate=pl.CostEstimate(
+            flops=3 * heads * seq_len * seq_len * HDIM,
+            bytes_accessed=4 * 2 * seq_len * heads * HDIM,
+            transcendentals=heads * seq_len * seq_len // 2,
+        ),
+    )(joined)
+
+
+def split_heads(hidden, down_weight, residual, ln_gain, ln_bias, qkv_weight):
+    inner = hidden[0]
+    seq_len, units = inner.shape
+    wide = lax.axis_size("wide")
+    wide_rows = seq_len // wide
+    part = wide_rows // CHUNKS
+    wide_at = lax.axis_index("wide")
+    narrow_at = lax.axis_index("narrow")
+    half = qkv_weight.shape[1] // 2
+    own_resid = lax.dynamic_slice_in_dim(residual[0], wide_at * wide_rows, wide_rows, 0)
+    inner = inner.reshape(wide, CHUNKS, part, units)
+    contract = (((1,), (1,)), ((), ()))
+    streams, joins = [], []
+    for chunk in range(CHUNKS):
+        rows = inner[:, chunk].reshape(wide * part, units)
+        partial_ffn = lax.dot_general(
+            rows, down_weight, contract, preferred_element_type=jnp.float32
+        ).astype(jnp.bfloat16)
+        summed = lax.psum_scatter(partial_ffn, "wide", scatter_dimension=0, tiled=True)
+        if chunk:
+            summed, arrived = lax.optimization_barrier((summed, arrived))
+        resid = own_resid[chunk * part : (chunk + 1) * part].astype(jnp.float32)
+        mine = (resid + summed.astype(jnp.float32)).astype(jnp.bfloat16)
+        streams.append(mine)
+        values = mine.astype(jnp.float32)
+        moments = jnp.stack([jnp.sum(values, axis=1), jnp.sum(values * values, axis=1)])
+        totals, squares = moments + from_behind(moments, "narrow", 1)
+        mean = totals / D
+        var = squares / D - mean * mean
+        normed = (
+            (values - mean[:, None]) * lax.rsqrt(var + 1e-05)[:, None] * ln_gain + ln_bias
+        ).astype(jnp.bfloat16)
+        arrived = from_behind(normed, "section", 1)
+        gathered = lax.all_gather(arrived, "wide", axis=0, tiled=True)
+        partial_qkv = jnp.dot(gathered, qkv_weight, preferred_element_type=jnp.float32)
+        other = lax.dynamic_slice_in_dim(partial_qkv, (1 - narrow_at) * half, half, 1)
+        own = lax.dynamic_slice_in_dim(partial_qkv, narrow_at * half, half, 1)
+        came = from_behind(other.astype(jnp.bfloat16), "narrow", 1)
+        joined = (own + came.astype(jnp.float32)).astype(jnp.bfloat16)
+        joins.append(joined.reshape(wide, part, half))
+    own_rows = jnp.concatenate(streams, axis=0)
+    joined = jnp.concatenate(joins, axis=1).reshape(seq_len, half)
+    attended = attention(joined)
+    query_count = seq_len // 2
+    away = lax.dynamic_slice_in_dim(attended, (1 - narrow_at) * query_count, query_count, 0)
+    home = lax.dynamic_slice_in_dim(attended, narrow_at * query_count, query_count, 0)
+    came = from_behind(away, "narrow", 1)
+    first = narrow_at == 0
+    attended = jnp.concatenate(
+        [jnp.where(first, home, came), jnp.where(first, came, home)], axis=1
+    )
+    return (own_rows[None], attended[None])
+
+
+def split_queries(hidden, down_weight, residual, ln_gain, ln_bias, qkv_weight):
     inner = hidden[0]
     resid = residual[0]
     seq_len = inner.shape[0]
@@ -61,6 +162,14 @@
     return (own_rows[None], attended[None])
 
 
+def per_device(hidden, down_weight, residual, ln_gain, ln_bias, qkv_weight):
+    heads_here = qkv_weight.shape[1] // (3 * HDIM)
+    wide_rows = hidden.shape[1] // lax.axis_size("wide")
+    even = heads_here % 2 == 0 and wide_rows % (16 * CHUNKS) == 0
+    plan = split_heads if lax.axis_size("narrow") == 2 and even else split_queries
+    return plan(hidden, down_weight, residual, ln_gain, ln_bias, qkv_weight)
+
+
 def solution(mesh):
     return jax.shard_map(
         per_device,

time: 1250 us -> 413 us (0.33)
  waiting for transfers between devices: 760 us -> 247 us
  blocking collectives: 290 us -> 0 us
  other arithmetic: 48.1 us -> 11.6 us
    psum x1 -> x0, waiting for transfers between devices: 493 us -> none  [per_device(): summed = lax.psum(partial_ffn, 'wide')]
    psum x2 -> x0, blocking collectives: 290 us -> none  [the longest x1 285 us: per_device(): lax.psum(jnp.dot(normed, qkv_weight, preferred_element_type=jnp.float32),...]
    ppermute x1 -> x7, waiting for transfers between devices: 267 us -> 76.7 us  [from_behind(): return lax.ppermute(value, axis, pairs)]
    reduce_scatter x0 -> x2, waiting for transfers between devices: none -> 92.9 us  [split_heads(): lax.psum_scatter(partial_ffn, 'wide', scatter_dimension=0, tiled=True)]
    all_gather x0 -> x2, waiting for transfers between devices: none -> 77.4 us  [split_heads(): gathered = lax.all_gather(arrived, 'wide', axis=0, tiled=True)]
    sub x1 -> x0, other arithmetic: 21.2 us -> none  [per_device(): expd = jnp.exp(scores - top)]
  transfers between devices with their start and end apart: 2 -> 11, of which waited for: 2 -> 10; matrix products, arithmetic and copies ran while one was open for 0% -> 21% of each run, Pallas kernels for 0% -> 0%
where the time goes in v1:
time: 413 us
  waiting for transfers between devices  247 us (60%)
  matrix products  104 us (25%)
  local copies, waits for them, and re-layouts  15.9 us (4%)
  between operations  13.9 us (3%)
  other arithmetic  11.6 us (3%)
  starting transfers between devices  10.9 us (3%)
  Pallas kernels  9.4 us (2%)
    reduce_scatter x2, waiting for transfers between devices, split_heads(): lax.psum_scatter(partial_ffn, 'wide', scatter_dimension=0, tiled=True)  92.9 us
    all_gather x2, waiting for transfers between devices, split_heads(): gathered = lax.all_gather(arrived, 'wide', axis=0, tiled=True)  77.4 us
    ppermute x7, waiting for transfers between devices, from_behind(): return lax.ppermute(value, axis, pairs)  76.7 us
    dot_general x2, matrix products, split_heads(): lax.dot_general(rows, down_weight, contract, preferred_element_type=jnp.f...  54 us
    dot_general x2, matrix products, split_heads(): jnp.dot(gathered, qkv_weight, preferred_element_type=jnp.float32)  49.7 us
    ppermute x7, starting transfers between devices, from_behind(): return lax.ppermute(value, axis, pairs)  10.6 us
    pallas_call x1, Pallas kernels, attention(): pl.pallas_call(functools.partial(attend_head, seq_len), grid=(heads,), in...  9.4 us
  transfers between devices with their start and end apart: 11, of which 10 were waited for; matrix products, arithmetic and copies ran while one was open for 21% of the time, Pallas kernels for 0%

profile of v1, /device:TPU:0, one launch (start us, length us, event | category | flops | bytes accessed | tf_op | source)
XLA Modules:
  0.0 412.7 jit_solution(17390277613982902635)
XLA Ops:
  7.2 0.0 reduce-scatter.3.cloned.1.call-start
  7.2 6.1 %fusion.20 = (bf16[8,1,64,3072]{3,2,1,0:T(8,128)(2,1)}, bf16[8,1,64,3072]{3,2,1,0:T(8,128)(2,1)}) fusion(bf16[8,2,64,3072]{3,2,1,0:T(8,128)(2,1)} %bitcast.55), kind=kLoop, calls=%fused_computation.46 | loop fusion | bytes 12582912 | tf_op jit(solution)/shard_map/slice | solution.py:77
  13.3 26.9 %convolution_convert_fusion.1 = bf16[512,6144]{1,0:T(8,128)(2,1)} fusion(bf16[512,3072]{1,0:T(8,128)(2,1)} %bitcast.59, bf16[6144,3072]{1,0:T(8,128)(2,1)} %param.7), kind=kOutput, calls=%fused_computation.1 | convolution fusion | flops 19330498560 | bytes 47185920 | tf_op jit(solution)/shard_map/dot_general | solution.py:78
  40.2 0.0 reduce-scatter.3.cloned.1.call-update
  40.2 0.0 reduce-scatter.5.cloned.1.call-start
  40.3 27.1 %convolution_convert_fusion = bf16[512,6144]{1,0:T(8,128)(2,1)} fusion(bf16[512,3072]{1,0:T(8,128)(2,1)} %bitcast.58, bf16[6144,3072]{1,0:T(8,128)(2,1)} %param.7), kind=kOutput, calls=%fused_computation | convolution fusion | flops 19330498560 | bytes 47185920 | tf_op jit(solution)/shard_map/dot_general | solution.py:78
  67.4 0.0 copy-start.5
  67.4 0.0 copy-start.6
  67.4 0.0 reduce-scatter.5.cloned.1.call-update
  67.4 0.0 all-gather.3.cloned.1.call-start
  67.4 45.5 %reduce-scatter.3.cloned.1.call-done = bf16[64,6144]{1,0:T(8,128)(2,1)} async-done(((bf16[512,6144]{1,0:T(8,128)(2,1)}), bf16[64,6144]{1,0:T(8,128)(2,1)}) %reduce-scatter.3.cloned.1.call-update) | async-done | bytes 786448 | tf_op jit(solution)/shard_map/reduce_scatter | solution.py:81
  112.9 1.8 convert_reduce_fusion.1
  114.7 1.5 collective-permute-start
  116.3 2.1 collective-permute-done
  118.4 0.0 copy-done.5
  118.4 0.0 copy-done.6
  118.4 0.3 fusion.4
  118.8 1.5 collective-permute-start.1
  120.3 14.5 %collective-permute-done.1 = bf16[64,6144]{1,0:T(8,128)(2,1)S(1)} collective-permute-done((bf16[64,6144]{1,0:T(8,128)(2,1)S(1)}, bf16[64,6144]{1,0:T(8,128)(2,1)S(1)}, u32[]{:S(2)}, u32[]{:S(2)}) %collective-permute-start.1) | collective-permute-done | bytes 786464 | tf_op jit(solution)/shard_map/ppermute | solution.py:19
  134.8 0.0 copy-start.3
  134.8 0.9 copy-done.3
  135.7 0.0 all-gather.3.cloned.1.call-update
  135.7 0.2 all-gather.5.cloned.1.call-start
  136.0 47.5 %reduce-scatter.5.cloned.1.call-done = bf16[64,6144]{1,0:T(8,128)(2,1)} async-done(((bf16[512,6144]{1,0:T(8,128)(2,1)}), bf16[64,6144]{1,0:T(8,128)(2,1)}) %reduce-scatter.5.cloned.1.call-update) | async-done | bytes 786448 | tf_op jit(solution)/shard_map/reduce_scatter | solution.py:81
  183.4 1.8 convert_reduce_fusion
  185.2 1.5 collective-permute-start.3
  186.8 2.1 collective-permute-done.3
  188.9 0.3 fusion.9
  189.3 1.5 collective-permute-start.4
  190.8 14.6 %collective-permute-done.4 = bf16[64,6144]{1,0:T(8,128)(2,1)S(1)} collective-permute-done((bf16[64,6144]{1,0:T(8,128)(2,1)S(1)}, bf16[64,6144]{1,0:T(8,128)(2,1)S(1)}, u32[]{:S(2)}, u32[]{:S(2)}) %collective-permute-start.4) | collective-permute-done | bytes 786464 | tf_op jit(solution)/shard_map/ppermute | solution.py:19
  205.4 0.0 copy-start.4
  205.4 0.9 copy-done.4
  206.3 0.0 all-gather.5.cloned.1.call-update
  206.3 42.3 %all-gather.3.cloned.1.call-done = bf16[512,6144]{1,0:T(8,128)(2,1)} async-done(((bf16[64,6144]{1,0:T(8,128)(2,1)}), bf16[512,6144]{1,0:T(8,128)(2,1)}) %all-gather.3.cloned.1.call-update) | async-done | bytes 6291472 | tf_op jit(solution)/shard_map/all_gather | solution.py:96
  248.6 24.8 %fusion.21 = f32[512,3072]{1,0:T(8,128)S(1)} fusion(bf16[512,6144]{1,0:T(8,128)(2,1)} %all-gather.3.cloned.1.call-done, bf16[6144,3072]{1,0:T(8,128)(2,1)} %param.11), kind=kOutput, calls=%fused_computation.47 | convolution fusion | flops 19327352832 | bytes 50331648 | tf_op jit(solution)/shard_map/dot_general | solution.py:97
  273.4 0.0 copy-start
  273.4 2.6 copy-done
  276.1 1.4 dynamic-slice_convert_fusion.1
  277.5 1.5 collective-permute-start.2
  278.9 35.2 %all-gather.5.cloned.1.call-done = bf16[512,6144]{1,0:T(8,128)(2,1)} async-done(((bf16[64,6144]{1,0:T(8,128)(2,1)}), bf16[512,6144]{1,0:T(8,128)(2,1)}) %all-gather.5.cloned.1.call-update) | async-done | bytes 6291472 | tf_op jit(solution)/shard_map/all_gather | solution.py:96
  314.1 24.8 %fusion.22 = f32[512,3072]{1,0:T(8,128)S(1)} fusion(bf16[512,6144]{1,0:T(8,128)(2,1)} %all-gather.5.cloned.1.call-done, bf16[6144,3072]{1,0:T(8,128)(2,1)} %param.11), kind=kOutput, calls=%fused_computation.48 | convolution fusion | flops 19327352832 | bytes 50331648 | tf_op jit(solution)/shard_map/dot_general | solution.py:97
  338.9 0.0 copy-start.1
  339.0 2.6 copy-done.1
  341.6 1.3 dynamic-slice_convert_fusion
  342.9 1.5 collective-permute-start.5
  344.4 0.0 copy-start.2
  344.4 0.0 collective-permute-done.2
  344.4 2.5 add_convert_fusion.1
  346.9 32.9 %collective-permute-done.5 = bf16[512,1536]{1,0:T(8,128)(2,1)} collective-permute-done((bf16[512,1536]{1,0:T(8,128)(2,1)}, bf16[512,1536]{1,0:T(8,128)(2,1)}, u32[]{:S(2)}, u32[]{:S(2)}) %collective-permute-start.5) | collective-permute-done | bytes 1572896 | tf_op jit(solution)/shard_map/ppermute | solution.py:19
  379.8 0.0 copy-done.2
  379.8 2.0 add_convert_fusion
  381.8 0.2 pad_maximum_fusion
  382.0 9.4 %shard_map.77 = bf16[1024,512]{1,0:T(8,128)(2,1)S(1)} custom-call(bf16[1024,1536]{1,0:T(8,128)(2,1)S(1)} %bitcast.54), custom_call_target="tpu_custom_call" | custom-call | flops 1610612736 | bytes 4194304 | tf_op jit(solution)/shard_map/pallas_call | solution.py:48
  391.5 1.5 collective-permute-start.6
  393.0 1.2 maximum_bitcast_fusion
  394.3 10.5 %collective-permute-done.6 = bf16[512,512]{1,0:T(8,128)(2,1)S(1)} collective-permute-done((bf16[512,512]{1,0:T(8,128)(2,1)S(1)}, bf16[512,512]{1,0:T(8,128)(2,1)S(1)}, u32[]{:S(2)}, u32[]{:S(2)}) %collective-permute-start.6) | collective-permute-done | bytes 524320 | tf_op jit(solution)/shard_map/ppermute | solution.py:19
  404.8 0.2 broadcast_select_fusion.1
  405.0 1.1 maximum_bitcast_fusion.1
  (9 shorter events, 0.1 us)
Async XLA Ops:
  7.2 105.8 %reduce-scatter.3.cloned.1.call-start = ((), (), s32[]{:S(2)}) async-start(), calls=%async_computation.2 | async-start | bytes 7077888 | tf_op jit(solution)/shard_map/reduce_scatter | solution.py:81
  40.2 143.2 %reduce-scatter.5.cloned.1.call-start = ((), (), s32[]{:S(2)}) async-start(), calls=%async_computation.3 | async-start | bytes 7077888 | tf_op jit(solution)/shard_map/reduce_scatter | solution.py:81
  67.4 51.1 %copy-start.5 = (f32[6144]{0:T(1024)S(1)}, f32[6144]{0:T(1024)}, u32[]{:S(2)}) copy-start(f32[6144]{0:T(1024)} %param.10) | copy-start | bytes 73732
  67.4 51.1 %copy-start.6 = (f32[6144]{0:T(1024)S(1)}, f32[6144]{0:T(1024)}, u32[]{:S(2)}) copy-start(f32[6144]{0:T(1024)} %param.9) | copy-start | bytes 73732
  67.4 181.2 %all-gather.3.cloned.1.call-start = ((), (), s32[]{:S(2)}) async-start(), calls=%async_computation.4 | async-start | bytes 7077888 | tf_op jit(solution)/shard_map/all_gather | solution.py:96
  114.7 3.6 collective-permute-start
  118.8 16.0 %collective-permute-start.1 = (bf16[64,6144]{1,0:T(8,128)(2,1)S(1)}, bf16[64,6144]{1,0:T(8,128)(2,1)S(1)}, u32[]{:S(2)}, u32[]{:S(2)}) collective-permute-start(bf16[64,6144]{1,0:T(8,128)(2,1)S(1)} %fusion.4), channel_id=1, source_target_pairs={{0,16},{16,0},{1,17},{17,1},{2,18},{18,2},{3,19},{19,3},{4,20},{20... | collective-permute-start | bytes 2359304 | tf_op jit(solution)/shard_map/ppermute | solution.py:19
  134.8 0.9 copy-start.3
  135.7 178.4 %all-gather.5.cloned.1.call-start = ((), (), s32[]{:S(2)}) async-start(), calls=%async_computation.5 | async-start | bytes 7077888 | tf_op jit(solution)/shard_map/all_gather | solution.py:96
  185.2 3.6 collective-permute-start.3
  189.3 16.1 %collective-permute-start.4 = (bf16[64,6144]{1,0:T(8,128)(2,1)S(1)}, bf16[64,6144]{1,0:T(8,128)(2,1)S(1)}, u32[]{:S(2)}, u32[]{:S(2)}) collective-permute-start(bf16[64,6144]{1,0:T(8,128)(2,1)S(1)} %fusion.9), channel_id=1, source_target_pairs={{0,16},{16,0},{1,17},{17,1},{2,18},{18,2},{3,19},{19,3},{4,20},{20... | collective-permute-start | bytes 2359304 | tf_op jit(solution)/shard_map/ppermute | solution.py:19
  205.4 0.9 copy-start.4
  273.4 2.7 copy-start
  277.5 66.9 %collective-permute-start.2 = (bf16[512,1536]{1,0:T(8,128)(2,1)}, bf16[512,1536]{1,0:T(8,128)(2,1)S(1)}, u32[]{:S(2)}, u32[]{:S(2)}) collective-permute-start(bf16[512,1536]{1,0:T(8,128)(2,1)} %dynamic-slice_convert_fusion.1), channel_id=1, source_target_pairs={{0,1},{1,0},{2,3},{3,2},{4,5},{5,4},{6,7},{7,6},{8,9},{9,8},{10,11... | collective-permute-start | bytes 4718600 | tf_op jit(solution)/shard_map/ppermute | solution.py:19
  338.9 2.6 copy-start.1
  342.9 36.9 %collective-permute-start.5 = (bf16[512,1536]{1,0:T(8,128)(2,1)}, bf16[512,1536]{1,0:T(8,128)(2,1)}, u32[]{:S(2)}, u32[]{:S(2)}) collective-permute-start(bf16[512,1536]{1,0:T(8,128)(2,1)} %dynamic-slice_convert_fusion), channel_id=1, source_target_pairs={{0,1},{1,0},{2,3},{3,2},{4,5},{5,4},{6,7},{7,6},{8,9},{9,8},{10,11... | collective-permute-start | bytes 4718600 | tf_op jit(solution)/shard_map/ppermute | solution.py:19
  344.4 35.4 %copy-start.2 = (f32[512,3072]{1,0:T(8,128)S(1)}, f32[512,3072]{1,0:T(8,128)}, u32[]{:S(2)}) copy-start(f32[512,3072]{1,0:T(8,128)} %copy-done.1) | copy-start | bytes 18874372
  391.5 13.3 %collective-permute-start.6 = (bf16[512,512]{1,0:T(8,128)(2,1)S(1)}, bf16[512,512]{1,0:T(8,128)(2,1)S(1)}, u32[]{:S(2)}, u32[]{:S(2)}) collective-permute-start(bf16[512,512]{1,0:T(8,128)(2,1)S(1)} %constant_dynamic-slice_fusion), channel_id=1, source_target_pairs={{0,1},{1,0},{2,3},{3,2},{4,5},{5,4},{6,7},{7,6},{8,9},{9,8},{10,11... | collective-permute-start | bytes 1572872 | tf_op jit(solution)/shard_map/ppermute | solution.py:19
Sparse Core Ops, SparseCore 0:
  40.4 72.5 reduce-scatter.2
  115.2 68.1 reduce-scatter.4
  185.6 62.8 all-gather.2
  250.7 63.3 all-gather.4
